TPU v7x, 32 devices: a whole 2x2x4 slice. The times are simulated.
32 devices in a mesh: tm: 16 (over z, x, core), rows: 2 (over y).
Axes of the slice: x: 2, y: 2, z: 4, core: 2. Of those that a mesh axis runs over, the one named last changes fastest.
Arguments:
- latents: bfloat16 [16, 16, 104, 384], P('tm', 'rows'), may hold values from -6 to 6
- norm_gain: float32 [384], replicated, may hold values from 0.1 to 1.9
- conv_weight: bfloat16 [3, 3, 3, 384, 384], replicated, may hold values from -0.0625 to 0.0625
- up_weight: bfloat16 [3, 384, 768], replicated, may hold values from -0.1875 to 0.1875
Outputs:
- upsampled: bfloat16 [32, 16, 104, 384], P('tm', 'rows')
All inputs are finite; a program needn't handle non-finite values.
Results may differ from a plain program's by a relative error of at most 0.0052.
Values may be sent and summed in bfloat16 or wider, within the bound.
A program may use at most 64 MiB of HBM per device.

v0:
```python
import functools

import jax
import jax.numpy as jnp
from jax import lax
from jax.experimental import pallas as pl
from jax.experimental.pallas import tpu as pltpu
from jax.sharding import PartitionSpec as P

EPS = 1e-06
MESH = pl.DeviceIdType.MESH
F32 = jnp.float32
BF16 = jnp.bfloat16


def kernel(nt, nr, lat, gain, convw, upw, out,
           own, raw_a, raw_b, act, wts, ups, acc, blk,
           own_sem, w_sem, u_sem,
           a_send, b_send, relay_send, a_recv, b_recv,
           p_send, p_recv, h_send, x_send, h_recv, k_send, k_recv):
    rows, cols, ch = own.shape
    wide = act.shape[2]
    half = rows // 2
    first = half + 1
    t = lax.axis_index("tm")
    r = lax.axis_index("rows")
    odd = lax.rem(t, 2)
    chip_odd = lax.rem(t // 2, 2)
    flip = lax.rem(r, 2)
    mate = t + 1 - 2 * odd

    def row_of(k):
        return k + flip * (rows - 1 - 2 * k)

    def seq(p):
        return jnp.where(p < first, p, jnp.where(p == first, rows - 1, p - 1))

    own_copy = pltpu.make_async_copy(lat.at[0], own, own_sem)
    own_copy.start()

    def w_copy(a, b, c):
        return pltpu.make_async_copy(
            convw.at[a, b, c],
            wts.at[a, b * ch:(b + 1) * ch, c * ch:(c + 1) * ch],
            w_sem.at[a, b, c],
        )

    for a in (2, 0, 1):
        for b in range(3):
            for c in range(3):
                w_copy(a, b, c).start()
    u_copy = pltpu.make_async_copy(upw, ups, u_sem)
    u_copy.start()

    edge = cols // 16 * 16
    act[:, :, edge:, :] = jnp.zeros((5, rows + 2, wide - edge, ch), BF16)
    act[:, 0] = jnp.zeros((5, wide, ch), BF16)
    act[:, rows + 1] = jnp.zeros((5, wide, ch), BF16)

    @pl.when(t < 2)
    def _():
        raw_a[...] = jnp.zeros_like(raw_a)

    @pl.when(t < 4)
    def _():
        raw_b[...] = jnp.zeros_like(raw_b)

    barrier = pltpu.get_barrier_semaphore()
    friends = []
    for d in (-4, -2, 2, 4):
        friends.append((t + d, r, jnp.logical_and(t + d >= 0, t + d < nt)))
    for d in (-1, 1):
        inside = jnp.logical_and(r + d >= 0, r + d < nr)
        friends.append((t, r + d, inside))
        friends.append((mate, r + d, inside))
    count = jnp.int32(1)
    pl.semaphore_signal(barrier, inc=1, device_id=(mate, r), device_id_type=MESH)
    for tt, rr, there in friends:
        count = count + there.astype(jnp.int32)

        @pl.when(there)
        def _():
            pl.semaphore_signal(barrier, inc=1, device_id=(tt, rr), device_id_type=MESH)

    pl.semaphore_wait(barrier, count)

    def remote(src, dst, send, recv, tt, rr):
        return pltpu.make_async_remote_copy(
            src_ref=src, dst_ref=dst, send_sem=send, recv_sem=recv,
            device_id=(tt, rr), device_id_type=MESH,
        )

    has_a = t >= 2
    has_b = t >= 4
    sends_a = jnp.logical_and(chip_odd == 0, t + 2 < nt)
    sends_b = t + 4 < nt
    relays = jnp.logical_and(chip_odd == 1, has_b)

    def a_copy(k):
        row = row_of(k)
        return remote(lat.at[0, row], raw_a.at[row], a_send.at[k], a_recv.at[k], t + 2, r)

    def b_copy(k):
        row = row_of(k)
        return remote(lat.at[0, row], raw_b.at[row], b_send.at[k], b_recv.at[k], t + 4, r)

    def relay_copy(k):
        row = row_of(k)
        return remote(raw_b.at[row], raw_a.at[row], relay_send.at[k], a_recv.at[k], t - 2, r)

    def begin(p, _):
        k = seq(p)

        @pl.when(sends_b)
        def _():
            b_copy(k).start()

        @pl.when(sends_a)
        def _():
            a_copy(k).start()
        return 0

    lax.fori_loop(0, rows, begin, 0)

    def mate_copy(slot, w, k):
        row = row_of(k) + 1
        return remote(act.at[slot, row], act.at[1 + 2 * w, row], p_send.at[w, k], p_recv.at[w, k], mate, r)

    def side(q):
        d = (2 * flip - 1) * (1 - 2 * q)
        there = jnp.logical_and(r + d >= 0, r + d < nr)
        up = (1 - d) // 2
        return d, there, 1 + (1 - up) * (rows - 1), up * (rows + 1)

    def halo_copy(slot, q):
        d, _, src, dst = side(q)
        return remote(act.at[slot, src], act.at[slot, dst], h_send.at[slot, q], h_recv.at[slot, q], t, r + d)

    def cross_copy(slot, w, q):
        d, _, src, dst = side(q)
        to = 1 + 2 * w
        return remote(act.at[slot, src], act.at[to, dst], x_send.at[w, q], h_recv.at[to, q], mate, r + d)

    def mated(slot):
        if slot == 4:
            return odd == 0, 1
        if slot == 2:
            return None, odd
        return odd == 1, 0

    def when(cond):
        return (lambda f: f()) if cond is None else pl.when(cond)

    def activate(source, slot, k):
        row = row_of(k)
        v = source[row].astype(F32)
        s = v * lax.rsqrt(jnp.mean(v * v, axis=-1, keepdims=True) + EPS) * gain[...]
        s = 0.5 * s
        act[slot, row + 1, :cols, :] = (s + s * jnp.tanh(s)).astype(BF16)
        cond, w = mated(slot)

        @when(cond)
        def _():
            mate_copy(slot, w, k).start()

        for q, kq in ((0, 0), (1, rows - 1)):
            there = side(q)[1]

            @pl.when(jnp.logical_and(k == kq, there))
            def _():
                halo_copy(slot, q).start()

                @when(cond)
                def _():
                    cross_copy(slot, w, q).start()

    def poll(k):
        @pl.when(has_b)
        def _():
            b_copy(k).wait_recv()

        @pl.when(relays)
        def _():
            relay_copy(k).start()

    def wait_halo(slot, q):
        @pl.when(side(q)[1])
        def _():
            halo_copy(slot, q).wait_recv()

    def out_row(h):
        return half * (h + flip * (1 - 2 * h))

    def multiply(idx, h):
        which = idx // 3
        tap = lax.rem(idx, 3)
        slot = tap + 2 * which
        o = out_row(h)
        lhs = jnp.concatenate(
            [act[slot, pl.ds(o + b, half)].reshape(half * wide, ch) for b in range(3)], axis=1)
        part = jnp.dot(lhs, wts[tap], preferred_element_type=F32)
        at = pl.ds(pl.multiple_of(o * wide, 16), half * wide)
        acc[which, at] += part

    own_copy.wait()

    def act_own(p, _):
        activate(own, 4, jnp.where(p == 0, 0, jnp.where(p == 1, rows - 1, p - 1)))
        return 0

    lax.fori_loop(0, rows, act_own, 0)
    acc[...] = jnp.zeros(acc.shape, F32)
    for b in range(3):
        for c in range(3):
            w_copy(2, b, c).wait()

    def mate_wait(w, h):
        def body(k, _):
            mate_copy(2, w, k).wait_recv()
            return 0
        lax.fori_loop(h * first, first + h * (rows - first), body, 0)

    def ready(idx, h):
        for late, slot, w in ((0, 0, None), (1, 1, 0), (4, 3, 1), (5, 4, None)):
            @pl.when(idx == late)
            def _():
                if w is not None:
                    mate_wait(w, h)
                wait_halo(slot, h)

    lag = 2
    steps = rows + lag

    def arrive(p, _):
        @pl.when(p < rows)
        def _():
            poll(seq(p))
            activate(raw_b, 0, seq(p))

        @pl.when(p >= lag)
        def _():
            k = seq(p - lag)

            @pl.when(has_a)
            def _():
                a_copy(k).wait_recv()

            activate(raw_a, 2, k)

        @pl.when(p == 2)
        def _():
            for a in (0, 1):
                for b in range(3):
                    for c in range(3):
                        w_copy(a, b, c).wait()

        base = p - first
        early = jnp.where(p < 2, 5, jnp.where(p == 2, 4 * odd - (1 - odd), -1))
        even_job = base + 1
        odd_job = jnp.where(base == -1, 0, jnp.where(base == 1, 2, jnp.where(base == 2, 1, jnp.where(base == 3, 3, -1))))
        late = jnp.where(odd == 1, odd_job, even_job)
        idx = jnp.where(base < -1, early, jnp.where(base > 3, -1, late))
        h = jnp.where(base < -1, lax.rem(p, 2), 0)

        @pl.when(idx >= 0)
        def _():
            @pl.when(base == 1)
            def _():
                wait_halo(2, 0)

            ready(idx, h)
            multiply(idx, h)
        return 0

    lax.fori_loop(0, steps, arrive, 0)
    wait_halo(2, 1)

    def finish(which, source):
        def body(row, _):
            at = pl.ds(pl.multiple_of(row * wide, 16), wide)
            left = pltpu.roll(acc[which, at, :ch], 1, 0)
            right = pltpu.roll(acc[which, at, 2 * ch:], wide - 1, 0)
            total = left + acc[which, at, ch:2 * ch] + right
            kept = total[:cols] + source[row].astype(F32)
            blk[2 * which, at] = jnp.concatenate([kept, total[cols:]], axis=0).astype(BF16)
            return 0
        lax.fori_loop(0, rows, body, 0)

    def block_copy(h):
        at = pl.ds(pl.multiple_of(out_row(h) * wide, 16), half * wide)
        return remote(blk.at[2 - 2 * odd, at], blk.at[1, at], k_send.at[h], k_recv.at[h], mate, r)

    def joined(slots, o):
        return jnp.concatenate(
            [act[slot, pl.ds(o + b, half)].reshape(half * wide, ch) for slot in slots for b in range(3)],
            axis=1)

    def last(j, _):
        o = out_row(1)
        at = pl.ds(pl.multiple_of(o * wide, 16), half * wide)

        @pl.when(j == odd)
        def _():
            mate_wait(1, 1)
            wait_halo(3, 1)
            taps = wts[0:2].reshape(6 * ch, 3 * ch)
            acc[1, at] += jnp.dot(joined((2, 3), o), taps, preferred_element_type=F32)
            finish(1, own)

        @pl.when(j != odd)
        def _():
            mate_wait(0, 1)
            wait_halo(0, 1)
            wait_halo(1, 1)
            taps = wts[...].reshape(9 * ch, 3 * ch)
            acc[0, at] = jnp.dot(joined((0, 1, 2), o), taps, preferred_element_type=F32)
            finish(0, raw_a)

        @pl.when(j == 0)
        def _():
            for h in range(2):
                block_copy(h).start()
        return 0

    lax.fori_loop(0, 2, last, 0)
    u_copy.wait()

    def upsample(h, _):
        block_copy(h).wait_recv()
        o = out_row(h)
        at = pl.ds(pl.multiple_of(o * wide, 16), half * wide)
        lhs = jnp.concatenate([blk[i, at] for i in range(3)], axis=1)
        y = jnp.dot(lhs, ups[...], preferred_element_type=F32)
        y = y.reshape(half, wide, 2 * ch)[:, :cols].astype(BF16)
        out[0, pl.ds(o, half)] = y[:, :, :ch]
        out[1, pl.ds(o, half)] = y[:, :, ch:]
        return 0

    lax.fori_loop(0, 2, upsample, 0)

    def ends(k, _):
        for cond, copy in ((sends_a, a_copy), (sends_b, b_copy), (relays, relay_copy)):
            @pl.when(cond)
            def _():
                copy(k).wait_send()
        for w in range(2):
            mate_copy(2, w, k).wait_send()
        return 0

    lax.fori_loop(0, rows, ends, 0)
    for q in range(2):
        @pl.when(side(q)[1])
        def _():
            for slot in (0, 2, 4):
                halo_copy(slot, q).wait_send()
            for w in range(2):
                cross_copy(2, w, q).wait_send()
        block_copy(q).wait_send()


def solution(mesh):
    nt, nr = mesh.shape["tm"], mesh.shape["rows"]

    def local(latents, norm_gain, conv_weight, up_weight):
        _, rows, cols, ch = latents.shape
        wide = (cols + 16) // 16 * 16
        dma = pltpu.SemaphoreType.DMA
        hbm = pl.BlockSpec(memory_space=pltpu.HBM)
        vmem = pl.BlockSpec(memory_space=pltpu.VMEM)
        return pl.pallas_call(
            functools.partial(kernel, nt, nr),
            out_shape=jax.ShapeDtypeStruct((2, rows, cols, ch), BF16),
            in_specs=[hbm, vmem, hbm, hbm],
            out_specs=vmem,
            scratch_shapes=[
                pltpu.VMEM((rows, cols, ch), BF16),
                pltpu.VMEM((rows, cols, ch), BF16),
                pltpu.VMEM((rows, cols, ch), BF16),
                pltpu.VMEM((5, rows + 2, wide, ch), BF16),
                pltpu.VMEM((3, 3 * ch, 3 * ch), BF16),
                pltpu.VMEM((3 * ch, 2 * ch), BF16),
                pltpu.VMEM((2, rows * wide, 3 * ch), F32),
                pltpu.VMEM((3, rows * wide, ch), BF16),
                dma, dma((3, 3, 3)), dma,
                dma((rows,)), dma((rows,)), dma((rows,)), dma((rows,)), dma((rows,)),
                dma((2, rows)), dma((2, rows)),
                dma((5, 2)), dma((2, 2)), dma((5, 2)),
                dma((2,)), dma((2,)),
            ],
            compiler_params=pltpu.CompilerParams(
                collective_id=0, has_side_effects=True, vmem_limit_bytes=52 << 20),
        )(latents, norm_gain, conv_weight, up_weight.reshape(3 * ch, 2 * ch))

    return jax.shard_map(
        local, mesh=mesh,
        in_specs=(P("tm", "rows", None, None), P(), P(), P()),
        out_specs=P("tm", "rows", None, None), check_vma=False,
    )
```

profile of v0, /device:TPU:29, one launch (start us, length us, event | category | flops | bytes accessed | tf_op | source)
XLA Modules:
  0.0 40.2 jit_solution(2729540062481748126)
XLA Ops:
  0.0 0.0 copy-start
  0.0 1.1 %copy-done = bf16[1,8,104,384]{3,2,1,0:T(8,128)(2,1)S(1)} copy-done((bf16[1,8,104,384]{3,2,1,0:T(8,128)(2,1)S(1)}, bf16[1,8,104,384]{3,2,1,0:T(8,128)(2,1)}, u32[]{:S(2)}) %copy-start) | copy-done | bytes 639000
  1.1 0.0 copy-start.1
  1.1 0.7 %copy-done.1 = f32[384]{0:T(512)S(1)} copy-done((f32[384]{0:T(512)S(1)}, f32[384]{0:T(512)}, u32[]{:S(2)}) %copy-start.1) | copy-done | bytes 1560
  1.8 37.4 %shard_map.46 = bf16[2,8,104,384]{3,2,1,0:T(8,128)(2,1)S(1)} custom-call(bf16[1,8,104,384]{3,2,1,0:T(8,128)(2,1)S(1)} %copy-done, f32[384]{0:T(512)S(1)} %copy-done.1, bf16[3,3,3,384,384]{4,3,2,1,0:T(8,128)(2,1)} %convw.1, bf16[1152,768]{1,0:T(8,128)(2,1)} %bitcast.1), custom_call_target="tpu_custom_call" | custom-call | tf_op jit(solution)/shard_map/pallas_call | solution.py:370
  39.2 1.0 %copy.6 = bf16[2,8,104,384]{3,2,1,0:T(8,128)(2,1)} copy(bf16[2,8,104,384]{3,2,1,0:T(8,128)(2,1)S(1)} %shard_map.46) | data formatting | bytes 2555904
Async XLA Ops:
  0.0 1.1 %copy-start = (bf16[1,8,104,384]{3,2,1,0:T(8,128)(2,1)S(1)}, bf16[1,8,104,384]{3,2,1,0:T(8,128)(2,1)}, u32[]{:S(2)}) copy-start(bf16[1,8,104,384]{3,2,1,0:T(8,128)(2,1)} %lat.1) | copy-start | bytes 1916932
  1.1 0.7 %copy-start.1 = (f32[384]{0:T(512)S(1)}, f32[384]{0:T(512)}, u32[]{:S(2)}) copy-start(f32[384]{0:T(512)} %gain.1) | copy-start | bytes 4612
where the time goes:
time: 40.4 us; the launch traced here: 40.2 us
  Pallas kernels  37.4 us (93%)
  local copies, waits for them, and re-layouts  2.81 us (7%)
    pallas_call x1, Pallas kernels, local(): pl.pallas_call(functools.partial(kernel, nt, nr), out_shape=jax.ShapeDtyp...  37.4 us
    unnamed x5, local copies, waits for them, and re-layouts  2.81 us

commit v1 on v0

--- a/solution.py
+++ b/solution.py
@@ -13,9 +13,9 @@
 BF16 = jnp.bfloat16
 
 
-def kernel(nt, nr, lat, gain, convw, upw, out,
-           own, raw_a, raw_b, act, wts, ups, acc, blk,
-           own_sem, w_sem, u_sem,
+def kernel(nt, nr, lat, gain_in, convw, upw, out,
+           own, gain, raw_a, raw_b, act, wts, ups, acc, blk,
+           own_sem, g_sem, w_sem, u_sem,
            a_send, b_send, relay_send, a_recv, b_recv,
            p_send, p_recv, h_send, x_send, h_recv, k_send, k_recv):
     rows, cols, ch = own.shape
@@ -37,6 +37,8 @@
 
     own_copy = pltpu.make_async_copy(lat.at[0], own, own_sem)
     own_copy.start()
+    gain_copy = pltpu.make_async_copy(gain_in, gain, g_sem)
+    gain_copy.start()
 
     def w_copy(a, b, c):
         return pltpu.make_async_copy(
@@ -203,6 +205,7 @@
         acc[which, at] += part
 
     own_copy.wait()
+    gain_copy.wait()
 
     def act_own(p, _):
         activate(own, 4, jnp.where(p == 0, 0, jnp.where(p == 1, rows - 1, p - 1)))
@@ -370,10 +373,11 @@
         return pl.pallas_call(
             functools.partial(kernel, nt, nr),
             out_shape=jax.ShapeDtypeStruct((2, rows, cols, ch), BF16),
-            in_specs=[hbm, vmem, hbm, hbm],
+            in_specs=[hbm, hbm, hbm, hbm],
             out_specs=vmem,
             scratch_shapes=[
                 pltpu.VMEM((rows, cols, ch), BF16),
+                pltpu.VMEM((ch,), F32),
                 pltpu.VMEM((rows, cols, ch), BF16),
                 pltpu.VMEM((rows, cols, ch), BF16),
                 pltpu.VMEM((5, rows + 2, wide, ch), BF16),
@@ -381,7 +385,7 @@
                 pltpu.VMEM((3 * ch, 2 * ch), BF16),
                 pltpu.VMEM((2, rows * wide, 3 * ch), F32),
                 pltpu.VMEM((3, rows * wide, ch), BF16),
-                dma, dma((3, 3, 3)), dma,
+                dma, dma, dma((3, 3, 3)), dma,
                 dma((rows,)), dma((rows,)), dma((rows,)), dma((rows,)), dma((rows,)),
                 dma((2, rows)), dma((2, rows)),
                 dma((5, 2)), dma((2, 2)), dma((5, 2)),
@@ -389,7 +393,8 @@
             ],
             compiler_params=pltpu.CompilerParams(
                 collective_id=0, has_side_effects=True, vmem_limit_bytes=52 << 20),
-        )(latents, norm_gain, conv_weight, up_weight.reshape(3 * ch, 2 * ch))
+        )(pltpu.with_memory_space_constraint(latents, pltpu.HBM), pltpu.with_memory_space_constraint(norm_gain, pltpu.HBM),
+          conv_weight, up_weight.reshape(3 * ch, 2 * ch))
 
     return jax.shard_map(
         local, mesh=mesh,

time: 40.4 us -> 37.8 us (0.936)
  local copies, waits for them, and re-layouts: 2.81 us -> 1.05 us
  Pallas kernels: 37.4 us -> 36.6 us
    unnamed x5 -> x1, local copies, waits for them, and re-layouts: 2.81 us -> 1.05 us
    pallas_call x1, Pallas kernels: 37.4 us -> 36.6 us  [local(): pl.pallas_call(functools.partial(kernel, nt, nr), out_shape=jax.ShapeDtyp...]
where the time goes in v1:
time: 37.8 us; the launch traced here: 37.6 us
  Pallas kernels  36.6 us (97%)
  local copies, waits for them, and re-layouts  1.05 us (3%)
    pallas_call x1, Pallas kernels, local(): pl.pallas_call(functools.partial(kernel, nt, nr), out_shape=jax.ShapeDtyp...  36.6 us
    unnamed x1, local copies, waits for them, and re-layouts  1.05 us

profile of v1, /device:TPU:29, one launch (start us, length us, event | category | flops | bytes accessed | tf_op | source)
XLA Modules:
  0.0 37.6 jit_solution(17694551428763137664)
XLA Ops:
  0.0 36.6 %shard_map.46 = bf16[2,8,104,384]{3,2,1,0:T(8,128)(2,1)S(1)} custom-call(bf16[1,8,104,384]{3,2,1,0:T(8,128)(2,1)} %lat.1, f32[384]{0:T(512)} %gain_in.1, bf16[3,3,3,384,384]{4,3,2,1,0:T(8,128)(2,1)} %convw.1, bf16[1152,768]{1,0:T(8,128)(2,1)} %bitcast.1), custom_call_target="tpu_custom_call" | custom-call | tf_op jit(solution)/shard_map/pallas_call | solution.py:373
  36.6 1.0 %copy.6 = bf16[2,8,104,384]{3,2,1,0:T(8,128)(2,1)} copy(bf16[2,8,104,384]{3,2,1,0:T(8,128)(2,1)S(1)} %shard_map.46) | data formatting | bytes 2555904
